TPU v7x, 32 devices: a whole 2x2x4 slice. The times are simulated.
32 devices in a mesh: row: 8 (over z, x), col: 4 (over y, core).
Axes of the slice: x: 2, y: 2, z: 4, core: 2. Of those that a mesh axis runs over, the one named last changes fastest.
Arguments:
- diag_inverse: bfloat16 [2, 8192, 8192], P(None, 'col', 'row'), as said below
- panel_rhs: bfloat16 [2, 8192, 128], P(None, 'row'), may hold values from -6 to 6
- below: bfloat16 [2, 22528, 8192], P(None, 'row', 'col'), may hold values from -0.03125 to 0.03125
- row_ids: int32 [2, 176], P(None, 'row'), may hold values from 0 to 256, as said below
- ancestor_rhs: bfloat16 [24576, 128], P(('row', 'col')), may hold values from -6 to 6
- ancestor_solution: bfloat16 [24576, 128], P(('row', 'col')), may hold values from -6 to 6
Outputs:
- solution: bfloat16 [2, 8192, 128], P(None, ('row', 'col'))
- rhs_updated: bfloat16 [24576, 128], P(('row', 'col'))
Inputs may be any that keep to these rules, and one draw needn't show every extreme that they name: diag_inverse[p] is lower triangular with a positive diagonal. `row_ids`: slots 22 r to 22 r + 21 of either panel belong to the r-th index of row. Each holds 256 (empty) or a later block row that this index owns: for panel 0 a panel-1 block row in [r * 8, r * 8 + 8) or a value in [64 + r * 24, 64 + r * 24 + 24); for panel 1 only the latter. Live ids of one panel are distinct. In each panel some index of row has all 22 slots live.
All inputs are finite; a program needn't handle non-finite values.
Results may differ from a plain program's by a relative error of at most 0.017.
Values may be sent and summed in bfloat16 or wider, within the bound.
A program may use at most 128 MiB of HBM per device.

v0:
```python
import jax
import jax.numpy as jnp
from jax import lax
from jax.sharding import PartitionSpec as P

BS = 128
NRHS = 128
PW = 64
CAP = 22
NA_R = 24


def on_device(diag_inverse, panel_rhs, below, row_ids, ancestor_rhs, ancestor_solution):
    row_count = lax.axis_size("row")
    row_place = lax.axis_index("row")
    col_place = lax.axis_index("col")
    panel_rows = PW // row_count
    contract_first = (((0,), (0,)), ((), ()))

    def row_total(partial_sum):
        return lax.psum(partial_sum.astype(jnp.bfloat16), "row").astype(jnp.float32)

    def col_total(partial_sum):
        return lax.psum(partial_sum.astype(jnp.bfloat16), "col").astype(jnp.float32)

    def pick_panel(slot_ids):
        position = slot_ids - row_place * panel_rows
        return (position[:, None] == jnp.arange(panel_rows)[None, :]) & (slot_ids[:, None] < PW)

    def pick_later(slot_ids):
        position = slot_ids - PW - row_place * NA_R
        return position[:, None] == jnp.arange(NA_R)[None, :]

    def to_rows(picked, slot_sums):
        placed = jnp.einsum(
            "sk,sbn->kbn", picked.astype(jnp.float32), slot_sums, precision=lax.Precision.HIGHEST
        )
        return placed.reshape(-1, NRHS)

    def slot_values(picked, source_rows):
        return jnp.einsum(
            "sk,kbn->sbn",
            picked.astype(jnp.bfloat16),
            source_rows,
            preferred_element_type=jnp.float32,
        )

    def transpose_product(panel_index, values):
        flat_values = values.astype(jnp.bfloat16).reshape(CAP * BS, NRHS)
        return lax.dot_general(
            below[panel_index], flat_values, contract_first, preferred_element_type=jnp.float32
        )

    def solve_back(forward_part, back_sum, panel_index):
        back_rhs = (forward_part.astype(jnp.float32) - back_sum).astype(jnp.bfloat16)
        return lax.dot_general(
            diag_inverse[panel_index], back_rhs, contract_first, preferred_element_type=jnp.float32
        )

    forward_zero = row_total(
        jnp.dot(diag_inverse[0], panel_rhs[0], preferred_element_type=jnp.float32)
    ).astype(jnp.bfloat16)
    slot_zero = jnp.dot(below[0], forward_zero, preferred_element_type=jnp.float32).reshape(
        CAP, BS, NRHS
    )
    panel_part = col_total(to_rows(pick_panel(row_ids[0]), slot_zero))
    panel_one_rhs = (panel_rhs[1].astype(jnp.float32) - panel_part).astype(jnp.bfloat16)
    forward_one = row_total(
        jnp.dot(diag_inverse[1], panel_one_rhs, preferred_element_type=jnp.float32)
    ).astype(jnp.bfloat16)
    later_zero = to_rows(pick_later(row_ids[0]), slot_zero)
    slot_one = jnp.dot(below[1], forward_one, preferred_element_type=jnp.float32).reshape(
        CAP, BS, NRHS
    )
    later_one = to_rows(pick_later(row_ids[1]), slot_one)

    def ancestor_share(partial_sum):
        return lax.psum_scatter(
            partial_sum.astype(jnp.bfloat16), "col", scatter_dimension=0, tiled=True
        ).astype(jnp.float32)

    update = ancestor_share(later_zero) + ancestor_share(later_one)
    rhs_updated = (ancestor_rhs.astype(jnp.float32) - update).astype(jnp.bfloat16)
    known_rows = lax.all_gather(ancestor_solution, "col", axis=0, tiled=True).reshape(
        NA_R, BS, NRHS
    )
    later_two = transpose_product(1, slot_values(pick_later(row_ids[1]), known_rows))
    ancestors_zero = slot_values(pick_later(row_ids[0]), known_rows)
    back_one = lax.psum(later_two.astype(jnp.bfloat16), "row").astype(jnp.float32)
    solution_one = col_total(solve_back(forward_one, back_one, 1)).astype(jnp.bfloat16)
    one_blocks = solution_one.reshape(panel_rows, BS, NRHS)
    values_zero = ancestors_zero + slot_values(pick_panel(row_ids[0]), one_blocks)
    back_zero = row_total(transpose_product(0, values_zero))
    share_rows = lax.psum_scatter(
        solve_back(forward_zero, back_zero, 0).astype(jnp.bfloat16),
        "col",
        scatter_dimension=0,
        tiled=True,
    )
    share_size = share_rows.shape[0]
    one_share = lax.dynamic_slice_in_dim(solution_one, col_place * share_size, share_size, 0)
    solution = jnp.stack([share_rows, one_share])
    return (solution, rhs_updated)


def solution(mesh):
    in_specs = (
        P(None, "col", "row"),
        P(None, "row", None),
        P(None, "row", "col"),
        P(None, "row"),
        P(("row", "col"), None),
        P(("row", "col"), None),
    )
    out_specs = (P(None, ("row", "col"), None), P(("row", "col"), None))
    return jax.shard_map(
        on_device, mesh=mesh, in_specs=in_specs, out_specs=out_specs, check_vma=False
    )
```

profile of v0, /device:TPU:0, one launch (start us, length us, event | category | flops | bytes accessed | tf_op | source)
XLA Modules:
  0.0 420.0 jit_solution(17048211158153917995)
XLA Ops:
  7.2 4.3 %fusion.30 = bf16[2048,128]{1,0:T(8,128)(2,1)} fusion(bf16[2,2048,1024]{2,1,0:T(8,128)(2,1)} %param.6, bf16[2,1024,128]{2,1,0:T(8,128)(2,1)} %param.7), kind=kOutput, calls=%fused_computation.26 | convolution fusion | flops 537133056 | bytes 4980736 | tf_op jit(solution)/shard_map/dot_general | solution.py:61
  11.6 10.1 %all_gather.3 = bf16[3072,128]{1,0:T(8,128)(2,1)S(1)} all-gather(bf16[768,128]{1,0:T(8,128)(2,1)S(1)} %copy-done.1), channel_id=1, replica_groups=mesh['row'=8,'col'=4] {'col'}, dimensions={0}, use_global_device_ids=true | all-gather | bytes 983040 | tf_op jit(solution)/shard_map/all_gather | solution.py:84
  22.6 64.5 %all-reduce.7.cloned.1.call-done = bf16[2048,128]{1,0:T(8,128)(2,1)} async-done(((bf16[2048,128]{1,0:T(8,128)(2,1)}), bf16[2048,128]{1,0:T(8,128)(2,1)}) %all-reduce.7.cloned.1.call-update) | async-done | bytes 524304 | tf_op jit(solution)/shard_map/psum | solution.py:21
  87.1 9.6 %fusion.20 = f32[2816,128]{0,1:T(8,128)} fusion(bf16[2048,128]{1,0:T(8,128)(2,1)} %all-reduce.7.cloned.1.call-done, bf16[2,2816,2048]{2,1,0:T(8,128)(2,1)} %param.8), kind=kOutput, calls=%fused_computation.20 | convolution fusion | flops 1476395008 | bytes 13500416 | tf_op jit(solution)/shard_map/dot_general | solution.py:63
  96.7 1.8 copy.17
  98.5 1.4 fusion.69
  100.7 6.8 %fusion.45 = bf16[2048,128]{0,1:T(8,128)(2,1)} fusion(bf16[2816,128]{1,0:T(8,128)(2,1)S(1)} %bitcast.120, bf16[2,2816,2048]{2,1,0:T(8,128)(2,1)} %param.8), kind=kOutput, calls=%fused_computation.31 | convolution fusion | flops 1476657152 | bytes 12779520 | tf_op jit(solution)/shard_map/dot_general | solution.py:50
  107.6 24.7 %all-reduce.9.cloned.1.call-done = bf16[1024,128]{1,0:T(8,128)(2,1)} async-done(((bf16[1024,128]{1,0:T(8,128)(2,1)}), bf16[1024,128]{1,0:T(8,128)(2,1)}) %all-reduce.9.cloned.1.call-update) | async-done | bytes 262160 | tf_op jit(solution)/shard_map/psum | solution.py:24
  132.3 4.6 %fusion.42 = bf16[2048,128]{0,1:T(8,128)(2,1)} fusion(bf16[2,2048,1024]{2,1,0:T(8,128)(2,1)} %param.6, bf16[1024,128]{1,0:T(8,128)(2,1)} %all-reduce.9.cloned.1.call-done, bf16[2,1024,128]{2,1,0:T(8,128)(2,1)S(1)} %copy-done.3), kind=kOutput, calls=%fused_computation.30 | convolution fusion | flops 537657344 | bytes 5242880 | tf_op jit(solution)/shard_map/dot_general | solution.py:69
  137.0 78.4 %all-reduce.15.cloned.1.call-done = (bf16[2048,128]{0,1:T(8,128)(2,1)}, bf16[2048,128]{0,1:T(8,128)(2,1)}) async-done(((bf16[2048,128]{0,1:T(8,128)(2,1)}, bf16[2048,128]{0,1:T(8,128)(2,1)}), (bf16[2048,128]{0,1:T(8,128)(2,1)}, bf16[2048,128]{0,1:T(8,128)(2,1)})) %all-reduce.15.cloned.1.call-update) | async-done | bytes 1048592 | tf_op jit(solution)/shard_map/psum | solution.py:89
  215.4 3.9 fusion.72
  219.6 31.8 %all-reduce.11.cloned.1.call-done = bf16[1024,128]{0,1:T(8,128)(2,1)} async-done(((bf16[1024,128]{0,1:T(8,128)(2,1)}), bf16[1024,128]{0,1:T(8,128)(2,1)}) %all-reduce.11.cloned.1.call-update) | async-done | bytes 262160 | tf_op jit(solution)/shard_map/psum | solution.py:24
  254.0 9.7 %fusion.48 = bf16[2048,128]{1,0:T(8,128)(2,1)} fusion(bf16[2816,128]{1,0:T(8,128)(2,1)S(1)} %bitcast.121, bf16[2,2816,2048]{2,1,0:T(8,128)(2,1)} %param.8), kind=kOutput, calls=%fused_computation.32 | convolution fusion | flops 1476657152 | bytes 12779520 | tf_op jit(solution)/shard_map/dot_general | solution.py:50
  263.8 72.8 %all-reduce.13.cloned.1.call-done = bf16[2048,128]{1,0:T(8,128)(2,1)} async-done(((bf16[2048,128]{1,0:T(8,128)(2,1)}), bf16[2048,128]{1,0:T(8,128)(2,1)}) %all-reduce.13.cloned.1.call-update) | async-done | bytes 524304 | tf_op jit(solution)/shard_map/psum | solution.py:21
  336.6 3.8 fusion.75
  340.5 1.6 fusion.57
  342.1 1.1 copy.26
  343.5 6.8 %fusion.23 = f32[2816,128]{0,1:T(8,128)S(1)} fusion(bf16[2048,128]{0,1:T(8,128)(2,1)} %get-tuple-element.7, bf16[2,2816,2048]{2,1,0:T(8,128)(2,1)} %param.8), kind=kOutput, calls=%fused_computation.21 | convolution fusion | flops 1476395008 | bytes 13500416 | tf_op jit(solution)/shard_map/dot_general | solution.py:72
  350.7 1.6 fusion.60
  352.3 1.1 copy.29
  354.3 5.5 %reduce-scatter.4.cloned.1.call-done = bf16[256,128]{0,1:T(8,128)(2,1)} async-done(((bf16[1024,128]{0,1:T(8,128)(2,1)}), bf16[256,128]{0,1:T(8,128)(2,1)}) %reduce-scatter.4.cloned.1.call-update) | async-done | bytes 65552 | tf_op jit(solution)/shard_map/reduce_scatter | solution.py:94
  361.4 24.2 %reduce-scatter.6.cloned.1.call-done = bf16[768,128]{1,0:T(8,128)(2,1)} async-done(((bf16[3072,128]{1,0:T(8,128)(2,1)}), bf16[768,128]{1,0:T(8,128)(2,1)}) %reduce-scatter.6.cloned.1.call-update) | async-done | bytes 196624 | tf_op jit(solution)/shard_map/reduce_scatter | solution.py:78
  385.6 25.8 %reduce-scatter.8.cloned.1.call-done = bf16[768,128]{1,0:T(8,128)(2,1)} async-done(((bf16[3072,128]{1,0:T(8,128)(2,1)}), bf16[768,128]{1,0:T(8,128)(2,1)}) %reduce-scatter.8.cloned.1.call-update) | async-done | bytes 196624 | tf_op jit(solution)/shard_map/reduce_scatter | solution.py:78
  411.3 1.8 subtract_convert_fusion.4
  (40 shorter events, 7.9 us)
Async XLA Ops:
  7.2 4.4 %copy-start.1 = (bf16[768,128]{1,0:T(8,128)(2,1)S(1)}, bf16[768,128]{1,0:T(8,128)(2,1)}, u32[]{:S(2)}) copy-start(bf16[768,128]{1,0:T(8,128)(2,1)} %param.11) | copy-start | bytes 589828
  7.2 14.6 %copy-start.2 = (s32[2,22]{1,0:T(2,128)S(1)}, s32[2,22]{1,0:T(2,128)}, u32[]{:S(2)}) copy-start(s32[2,22]{1,0:T(2,128)} %param.9) | copy-start | bytes 532
  7.2 79.9 %all-reduce.7.cloned.1.call-start = ((), (), s32[]{:S(2)}) async-start(), calls=%async_computation.3 | async-start | bytes 1048576 | tf_op jit(solution)/shard_map/psum | solution.py:21
  11.6 120.7 %all-reduce.9.cloned.1.call-start = ((), (), s32[]{:S(2)}) async-start(), calls=%async_computation.4 | async-start | bytes 524288 | tf_op jit(solution)/shard_map/psum | solution.py:24
  100.7 114.7 %all-reduce.15.cloned.1.call-start = ((), (), s32[]{:S(2)}) async-start(), calls=%async_computation.10 | async-start | bytes 2097152 | tf_op jit(solution)/shard_map/psum | solution.py:89
  100.7 31.6 %copy-start.3 = (bf16[2,1024,128]{2,1,0:T(8,128)(2,1)S(1)}, bf16[2,1024,128]{2,1,0:T(8,128)(2,1)}, u32[]{:S(2)}) copy-start(bf16[2,1024,128]{2,1,0:T(8,128)(2,1)} %param.7) | copy-start | bytes 1572868
  137.0 114.5 %all-reduce.11.cloned.1.call-start = ((), (), s32[]{:S(2)}) async-start(), calls=%async_computation.5 | async-start | bytes 524288 | tf_op jit(solution)/shard_map/psum | solution.py:24
  219.4 117.2 %all-reduce.13.cloned.1.call-start = ((), (), s32[]{:S(2)}) async-start(), calls=%async_computation.6 | async-start | bytes 1048576 | tf_op jit(solution)/shard_map/psum | solution.py:21
  254.0 82.6 %copy-start.4 = (bf16[2048,128]{1,0:T(8,128)(2,1)S(1)}, bf16[2048,128]{1,0:T(8,128)(2,1)}, u32[]{:S(2)}) copy-start(bf16[2048,128]{1,0:T(8,128)(2,1)} %all-reduce.7.cloned.1.call-done) | copy-start | bytes 1572868
  263.8 96.0 %reduce-scatter.4.cloned.1.call-start = ((), (), s32[]{:S(2)}) async-start(), calls=%async_computation.7 | async-start | bytes 327680 | tf_op jit(solution)/shard_map/reduce_scatter | solution.py:94
  340.4 45.1 %reduce-scatter.6.cloned.1.call-start = ((), (), s32[]{:S(2)}) async-start(), calls=%async_computation.8 | async-start | bytes 983040 | tf_op jit(solution)/shard_map/reduce_scatter | solution.py:78
  343.2 68.1 %reduce-scatter.8.cloned.1.call-start = ((), (), s32[]{:S(2)}) async-start(), calls=%async_computation.9 | async-start | bytes 983040 | tf_op jit(solution)/shard_map/reduce_scatter | solution.py:78
  350.3 61.1 %copy-start = (bf16[768,128]{1,0:T(8,128)(2,1)S(1)}, bf16[768,128]{1,0:T(8,128)(2,1)}, u32[]{:S(2)}) copy-start(bf16[768,128]{1,0:T(8,128)(2,1)} %param.10) | copy-start | bytes 589828
Sparse Core Ops, SparseCore 0:
  11.7 75.3 all-reduce.6
  100.8 31.4 all-reduce.8
  137.1 78.2 all-reduce.14
  219.5 31.9 all-reduce.10
  263.9 72.6 all-reduce.12
  340.5 19.2 reduce-scatter.3
  362.3 23.1 reduce-scatter.5
  388.1 23.1 reduce-scatter.7
where the time goes:
time: 420 us
  waiting for transfers between devices  328 us (78%)
  matrix products  56.1 us (13%)
  between operations  14.3 us (3%)
  blocking collectives  10.1 us (2%)
  local copies, waits for them, and re-layouts  8.26 us (2%)
    psum x2, waiting for transfers between devices, row_total(): return lax.psum(partial_sum.astype(jnp.bfloat16), 'row').astype(jnp.float32)  137 us
    psum x1, waiting for transfers between devices, on_device(): lax.psum(later_two.astype(jnp.bfloat16), 'row').astype(jnp.float32)  78.4 us
    psum x2, waiting for transfers between devices, col_total(): return lax.psum(partial_sum.astype(jnp.bfloat16), 'col').astype(jnp.float32)  56.6 us
    reduce_scatter x2, waiting for transfers between devices, ancestor_share(): lax.psum_scatter(partial_sum.astype(jnp.bfloat16), 'col', scatter_dimensi...  49.9 us
    dot_general x2, matrix products, transpose_product(): lax.dot_general(below[panel_index], flat_values, contract_first, preferre...  16.6 us
    all_gather x1, blocking collectives, on_device(): lax.all_gather(ancestor_solution, 'col', axis=0, tiled=True)  10.1 us
    dot_general x1, matrix products, on_device(): jnp.dot(below[0], forward_zero, preferred_element_type=jnp.float32)  9.59 us
  transfers between devices with their start and end apart: 8, of which 8 were waited for; matrix products, arithmetic and copies ran while one was open for 5% of the time, Pallas kernels for 0%

commit v1 on v0

--- a/solution.py
+++ b/solution.py
@@ -10,6 +10,11 @@
 NA_R = 24
 
 
+def add_all(x, name):
+    parts = lax.all_gather(x, name)
+    return jnp.sum(parts, axis=0)
+
+
 def on_device(diag_inverse, panel_rhs, below, row_ids, ancestor_rhs, ancestor_solution):
     row_count = lax.axis_size("row")
     row_place = lax.axis_index("row")
@@ -18,7 +23,7 @@
     contract_first = (((0,), (0,)), ((), ()))
 
     def row_total(partial_sum):
-        return lax.psum(partial_sum.astype(jnp.bfloat16), "row").astype(jnp.float32)
+        return add_all(partial_sum.astype(jnp.bfloat16), "row").astype(jnp.float32)
 
     def col_total(partial_sum):
         return lax.psum(partial_sum.astype(jnp.bfloat16), "col").astype(jnp.float32)

time: 420 us -> 482 us (1.15)
  waiting for transfers between devices: 328 us -> 380 us
  other arithmetic: 2.65 us -> 12 us
  local copies, waits for them, and re-layouts: 8.26 us -> 17.1 us
  matrix products: 56.1 us -> 50.1 us
    all_gather x0 -> x3, waiting for transfers between devices: none -> 193 us  [add_all(): parts = lax.all_gather(x, name)]
    psum x2 -> x0, waiting for transfers between devices: 137 us -> none  [row_total(): return lax.psum(partial_sum.astype(jnp.bfloat16), 'row').astype(jnp.float32)]
    reduce_scatter x1, waiting for transfers between devices: 5.5 us -> 20.8 us  [on_device(): lax.psum_scatter(solve_back(forward_zero, back_zero, 0).astype(jnp.bfloat...]
    reduce_scatter x2, waiting for transfers between devices: 49.9 us -> 37 us  [ancestor_share(): lax.psum_scatter(partial_sum.astype(jnp.bfloat16), 'col', scatter_dimensi...]
    psum x1, waiting for transfers between devices: 78.4 us -> 66.5 us  [on_device(): lax.psum(later_two.astype(jnp.bfloat16), 'row').astype(jnp.float32)]
    unnamed x12, local copies, waits for them, and re-layouts: 1.78 us -> 11.7 us
    reduce_sum x0 -> x3, other arithmetic: none -> 9.38 us  [add_all(): return jnp.sum(parts, axis=0)]
    psum x2, waiting for transfers between devices: 56.6 us -> 62.5 us  [col_total(): return lax.psum(partial_sum.astype(jnp.bfloat16), 'col').astype(jnp.float32)]
  transfers between devices with their start and end apart: 8 -> 9, of which waited for: 8 -> 9; matrix products, arithmetic and copies ran while one was open for 5% -> 9% of each run, Pallas kernels for 0% -> 0%
where the time goes in v1:
time: 482 us; the launch traced here: 481 us
  waiting for transfers between devices  380 us (79%)
  matrix products  50.1 us (10%)
  local copies, waits for them, and re-layouts  17.1 us (4%)
  between operations  14.1 us (3%)
  other arithmetic  12 us (2%)
  blocking collectives  7.22 us (1%)
    all_gather x3, waiting for transfers between devices, add_all(): parts = lax.all_gather(x, name)  193 us
    psum x1, waiting for transfers between devices, on_device(): lax.psum(later_two.astype(jnp.bfloat16), 'row').astype(jnp.float32)  66.5 us
    psum x2, waiting for transfers between devices, col_total(): return lax.psum(partial_sum.astype(jnp.bfloat16), 'col').astype(jnp.float32)  62.5 us
    reduce_scatter x2, waiting for transfers between devices, ancestor_share(): lax.psum_scatter(partial_sum.astype(jnp.bfloat16), 'col', scatter_dimensi...  37 us
    reduce_scatter x1, waiting for transfers between devices, on_device(): lax.psum_scatter(solve_back(forward_zero, back_zero, 0).astype(jnp.bfloat...  20.8 us
    dot_general x2, matrix products, transpose_product(): lax.dot_general(below[panel_index], flat_values, contract_first, preferre...  13.7 us
    unnamed x12, local copies, waits for them, and re-layouts  11.7 us
  transfers between devices with their start and end apart: 9, of which 9 were waited for; matrix products, arithmetic and copies ran while one was open for 9% of the time, Pallas kernels for 0%

profile of v1, /device:TPU:0, one launch (start us, length us, event | category | flops | bytes accessed | tf_op | source)
XLA Modules:
  0.0 481.3 jit_solution(14294825244280828900)
XLA Ops:
  7.2 4.3 fusion.30
  11.6 75.6 %all-gather.7.cloned.1.call-done = bf16[16384,128]{1,0:T(8,128)(2,1)} async-done(((bf16[2048,128]{1,0:T(8,128)(2,1)}), bf16[16384,128]{1,0:T(8,128)(2,1)}) %all-gather.7.cloned.1.call-update) | async-done | bytes 4194320 | tf_op jit(solution)/shard_map/all_gather | solution.py:14
  87.2 3.1 reduce_sum.36
  90.2 6.6 %fusion.20 = f32[2816,128]{0,1:T(8,128)S(1)} fusion(bf16[2048,128]{1,0:T(8,128)(2,1)S(1)} %reduce_sum.36, bf16[2,2816,2048]{2,1,0:T(8,128)(2,1)} %param.8), kind=kOutput, calls=%fused_computation.22 | convolution fusion | flops 1476395008 | bytes 13500416 | tf_op jit(solution)/shard_map/dot_general | solution.py:68
  99.6 30.9 %all-reduce.4.cloned.1.call-done = bf16[1024,128]{1,0:T(8,128)(2,1)} async-done(((bf16[1024,128]{1,0:T(8,128)(2,1)}), bf16[1024,128]{1,0:T(8,128)(2,1)}) %all-reduce.4.cloned.1.call-update) | async-done | bytes 262160 | tf_op jit(solution)/shard_map/psum | solution.py:29
  130.5 4.7 fusion.42
  135.3 7.2 %all_gather.23 = bf16[3072,128]{1,0:T(8,128)(2,1)S(1)} all-gather(bf16[768,128]{1,0:T(8,128)(2,1)S(1)} %copy-done.2), channel_id=1, replica_groups=mesh['row'=8,'col'=4] {'col'}, dimensions={0}, use_global_device_ids=true | all-gather | bytes 983040 | tf_op jit(solution)/shard_map/all_gather | solution.py:89
  143.4 7.0 %fusion.45 = bf16[2048,128]{0,1:T(8,128)(2,1)} fusion(bf16[2816,128]{1,0:T(8,128)(2,1)S(1)} %bitcast.134, bf16[2,2816,2048]{2,1,0:T(8,128)(2,1)} %param.8), kind=kOutput, calls=%fused_computation.33 | convolution fusion | flops 1476657152 | bytes 12779520 | tf_op jit(solution)/shard_map/dot_general | solution.py:55
  150.6 57.6 %all-gather.9.cloned.1.call-done = bf16[16384,128]{0,1:T(8,128)(2,1)} async-done(((bf16[2048,128]{0,1:T(8,128)(2,1)}), bf16[16384,128]{0,1:T(8,128)(2,1)}) %all-gather.9.cloned.1.call-update) | async-done | bytes 4194320 | tf_op jit(solution)/shard_map/all_gather | solution.py:14
  208.1 5.0 %copy.68 = bf16[16,8,8,2048]{3,2,1,0:T(8,128)(2,1)S(1)} copy(bf16[16,8,8,2048]{3,1,2,0:T(8,128)(2,1)} %bitcast.129) | data formatting | bytes 8388608
  213.1 3.2 bitcast_reduce_fusion.1
  216.3 66.5 %all-reduce.6.cloned.1.call-done = bf16[2048,128]{0,1:T(8,128)(2,1)} async-done(((bf16[2048,128]{0,1:T(8,128)(2,1)}), bf16[2048,128]{0,1:T(8,128)(2,1)}) %all-reduce.6.cloned.1.call-update) | async-done | bytes 524304 | tf_op jit(solution)/shard_map/psum | solution.py:94
  282.8 3.8 fusion.72
  286.6 31.6 %all-reduce.8.cloned.1.call-done = bf16[1024,128]{0,1:T(8,128)(2,1)} async-done(((bf16[1024,128]{0,1:T(8,128)(2,1)}), bf16[1024,128]{0,1:T(8,128)(2,1)}) %all-reduce.8.cloned.1.call-update) | async-done | bytes 262160 | tf_op jit(solution)/shard_map/psum | solution.py:29
  320.8 6.8 %fusion.48 = bf16[2048,128]{0,1:T(8,128)(2,1)} fusion(bf16[2816,128]{1,0:T(8,128)(2,1)S(1)} %bitcast.135, bf16[2,2816,2048]{2,1,0:T(8,128)(2,1)} %param.8), kind=kOutput, calls=%fused_computation.34 | convolution fusion | flops 1476657152 | bytes 12779520 | tf_op jit(solution)/shard_map/dot_general | solution.py:55
  330.6 6.7 %fusion.23 = f32[2816,128]{0,1:T(8,128)S(1)} fusion(bf16[2048,128]{0,1:T(8,128)(2,1)} %copy-done, bf16[2,2816,2048]{2,1,0:T(8,128)(2,1)} %param.8), kind=kOutput, calls=%fused_computation.23 | convolution fusion | flops 1476395008 | bytes 13500416 | tf_op jit(solution)/shard_map/dot_general | solution.py:77
  340.6 59.9 %all-gather.11.cloned.1.call-done = bf16[16384,128]{0,1:T(8,128)(2,1)} async-done(((bf16[2048,128]{0,1:T(8,128)(2,1)}), bf16[16384,128]{0,1:T(8,128)(2,1)}) %all-gather.11.cloned.1.call-update) | async-done | bytes 4194320 | tf_op jit(solution)/shard_map/all_gather | solution.py:14
  400.5 5.0 %copy.70 = bf16[16,8,8,2048]{3,2,1,0:T(8,128)(2,1)S(1)} copy(bf16[16,8,8,2048]{3,1,2,0:T(8,128)(2,1)} %bitcast.128) | data formatting | bytes 8388608
  405.5 3.2 bitcast_reduce_fusion
  408.9 3.7 fusion.75
  413.5 11.3 %reduce-scatter.6.cloned.1.call-done = bf16[768,128]{1,0:T(8,128)(2,1)} async-done(((bf16[3072,128]{1,0:T(8,128)(2,1)}), bf16[768,128]{1,0:T(8,128)(2,1)}) %reduce-scatter.6.cloned.1.call-update) | async-done | bytes 196624 | tf_op jit(solution)/shard_map/reduce_scatter | solution.py:83
  424.8 25.8 %reduce-scatter.8.cloned.1.call-done = bf16[768,128]{1,0:T(8,128)(2,1)} async-done(((bf16[3072,128]{1,0:T(8,128)(2,1)}), bf16[768,128]{1,0:T(8,128)(2,1)}) %reduce-scatter.8.cloned.1.call-update) | async-done | bytes 196624 | tf_op jit(solution)/shard_map/reduce_scatter | solution.py:83
  450.6 1.8 subtract_convert_fusion.4
  452.3 20.8 %reduce-scatter.4.cloned.1.call-done = bf16[256,128]{0,1:T(8,128)(2,1)} async-done(((bf16[1024,128]{0,1:T(8,128)(2,1)}), bf16[256,128]{0,1:T(8,128)(2,1)}) %reduce-scatter.4.cloned.1.call-update) | async-done | bytes 65552 | tf_op jit(solution)/shard_map/reduce_scatter | solution.py:99
  (47 shorter events, 15.5 us)
Async XLA Ops:
  7.2 4.4 copy-start.3
  7.2 80.0 %all-gather.7.cloned.1.call-start = ((), (), s32[]{:S(2)}) async-start(), calls=%async_computation.9 | async-start | bytes 4718592 | tf_op jit(solution)/shard_map/all_gather | solution.py:14
  11.5 119.0 %all-reduce.4.cloned.1.call-start = ((), (), s32[]{:S(2)}) async-start(), calls=%async_computation.3 | async-start | bytes 524288 | tf_op jit(solution)/shard_map/psum | solution.py:29
  98.7 36.5 %copy-start.2 = (bf16[768,128]{1,0:T(8,128)(2,1)S(1)}, bf16[768,128]{1,0:T(8,128)(2,1)}, u32[]{:S(2)}) copy-start(bf16[768,128]{1,0:T(8,128)(2,1)} %param.11) | copy-start | bytes 589828
  99.5 108.6 %all-gather.9.cloned.1.call-start = ((), (), s32[]{:S(2)}) async-start(), calls=%async_computation.10 | async-start | bytes 4718592 | tf_op jit(solution)/shard_map/all_gather | solution.py:14
  135.2 147.6 %all-reduce.6.cloned.1.call-start = ((), (), s32[]{:S(2)}) async-start(), calls=%async_computation.4 | async-start | bytes 1048576 | tf_op jit(solution)/shard_map/psum | solution.py:94
  150.4 167.9 %all-reduce.8.cloned.1.call-start = ((), (), s32[]{:S(2)}) async-start(), calls=%async_computation.5 | async-start | bytes 524288 | tf_op jit(solution)/shard_map/psum | solution.py:29
  216.3 101.9 %copy-start = (bf16[2048,128]{0,1:T(8,128)(2,1)}, bf16[2048,128]{0,1:T(8,128)(2,1)S(1)}, u32[]{:S(2)}) copy-start(bf16[2048,128]{0,1:T(8,128)(2,1)S(1)} %bitcast_reduce_fusion.1) | copy-start | bytes 1572868
  286.6 113.9 %all-gather.11.cloned.1.call-start = ((), (), s32[]{:S(2)}) async-start(), calls=%async_computation.11 | async-start | bytes 4718592 | tf_op jit(solution)/shard_map/all_gather | solution.py:14
  327.6 97.2 %reduce-scatter.6.cloned.1.call-start = ((), (), s32[]{:S(2)}) async-start(), calls=%async_computation.7 | async-start | bytes 983040 | tf_op jit(solution)/shard_map/reduce_scatter | solution.py:83
  330.3 120.2 %reduce-scatter.8.cloned.1.call-start = ((), (), s32[]{:S(2)}) async-start(), calls=%async_computation.8 | async-start | bytes 983040 | tf_op jit(solution)/shard_map/reduce_scatter | solution.py:83
  340.5 132.6 %reduce-scatter.4.cloned.1.call-start = ((), (), s32[]{:S(2)}) async-start(), calls=%async_computation.6 | async-start | bytes 327680 | tf_op jit(solution)/shard_map/reduce_scatter | solution.py:99
  408.6 41.9 %copy-start.1 = (bf16[768,128]{1,0:T(8,128)(2,1)S(1)}, bf16[768,128]{1,0:T(8,128)(2,1)}, u32[]{:S(2)}) copy-start(bf16[768,128]{1,0:T(8,128)(2,1)} %param.10) | copy-start | bytes 589828
Sparse Core Ops, SparseCore 0:
  11.6 75.4 all-gather.6
  99.6 30.8 all-reduce.3
  135.3 72.7 all-gather.8
  211.4 71.3 all-reduce.5
  286.7 31.4 all-reduce.7
  327.7 72.7 all-gather.10
  403.0 21.7 reduce-scatter.5
  427.3 23.1 reduce-scatter.7
  453.0 20.0 reduce-scatter.3
